TPU v7x, 256 devices: a whole 4x4x8 slice. The times are simulated.
256 devices in a mesh: section: 4 (over z_lo), dp: 64 (over x, y, z_hi, core).
Axes of the slice: x: 4, y: 4, z: 8 (z_hi: 2, z_lo: 4; z = z_hi * 4 + z_lo), core: 2. Of those that a mesh axis runs over, the one named last changes fastest.
Arguments:
- section_inputs: bfloat16 [4, 12544, 2048], P('section', 'dp'), may hold values from -16 to 16
- norm_gain: float32 [4, 2048], P('section'), may hold values from 0.25 to 1.75
- query_gain: float32 [4, 2048], P('section'), may hold values from -5 to 5
- key_gain: float32 [4, 2048], P('section'), may hold values from -5 to 5
- output_weight: bfloat16 [4, 2048, 2048], P('section', 'dp'), may hold values from -0.125 to 0.125
- full_sequence_gradient: bfloat16 [256, 196, 2048], P('dp'), may hold values from -6 to 6
- patch_order: int32 [256, 196], P('dp'), may hold values from 0 to 195, each once within a row
Outputs:
- input_grads: bfloat16 [4, 12544, 2048], P('section', 'dp')
- weight_grads: float32 [4, 2048, 2048], P('section', 'dp')
- gain_grads: float32 [4, 3, 2048], P('section')
Inputs may be any that keep to these rules, and one draw needn't show every extreme that they name: `patch_order`: each row holds every patch number once; the first 49 are the kept patches.
All inputs are finite; a program needn't handle non-finite values.
Results may differ from a plain program's by a relative error of at most 0.0057.
Values may be sent and summed in bfloat16 or wider, within the bound.
A program may use at most 128 MiB of HBM per device.

v0:
```python
import math
import jax
import jax.numpy as jnp
from jax import lax
from jax.sharding import PartitionSpec as P

HEADS = 16
KEPT = 49
PATCHES = 196
MICRO = 2
highest = lax.Precision.HIGHEST


def from_behind(block, axis, distance):
    devices = range(lax.axis_size(axis))
    route = [(i - distance, i) for i in devices if i - distance in devices]
    return lax.ppermute(block, axis, route)


def normalize(inputs):
    values = inputs.astype(jnp.float32)
    centred = values - jnp.mean(values, axis=-1, keepdims=True)
    variance = jnp.mean(centred * centred, axis=-1, keepdims=True)
    inverse = lax.rsqrt(variance + 1e-06)
    return (centred * inverse, inverse)


def attend_forward(normed, gain_row, query_row, key_row, heads):
    row_count, feature_width = normed.shape
    head_width = feature_width // heads
    split_shape = (row_count // KEPT, KEPT, heads, head_width)
    hidden = normed * gain_row
    queries = (hidden * query_row).reshape(split_shape)
    key_rows = (hidden * key_row).reshape(split_shape)
    value_rows = hidden.reshape(split_shape)
    attention_logits = jnp.einsum(
        "bqhd,bkhd->bhqk", queries, key_rows, precision=highest
    ) / math.sqrt(head_width)
    softmaxed = jax.nn.softmax(attention_logits, axis=-1)
    mixed = jnp.einsum("bhqk,bkhd->bqhd", softmaxed, value_rows, precision=highest)
    return (
        hidden,
        queries,
        key_rows,
        value_rows,
        softmaxed,
        mixed.reshape(row_count, feature_width).astype(jnp.bfloat16),
    )


def attend_backward(
    cotangent,
    back,
    normed,
    inverse,
    hidden,
    queries,
    key_rows,
    value_rows,
    softmaxed,
    gain_row,
    query_row,
    key_row,
):
    row_count, feature_width = back.shape
    head_width = queries.shape[-1]
    back_split = back.reshape(queries.shape)
    soft_grad = jnp.einsum("bqhd,bkhd->bhqk", back_split, value_rows, precision=highest)
    value_grad = jnp.einsum("bhqk,bqhd->bkhd", softmaxed, back_split, precision=highest).reshape(
        row_count, feature_width
    )
    score_grad = (
        softmaxed
        * (soft_grad - jnp.sum(soft_grad * softmaxed, axis=-1, keepdims=True))
        / math.sqrt(head_width)
    )
    query_grad = jnp.einsum("bhqk,bkhd->bqhd", score_grad, key_rows, precision=highest).reshape(
        row_count, feature_width
    )
    key_grad = jnp.einsum("bhqk,bqhd->bkhd", score_grad, queries, precision=highest).reshape(
        row_count, feature_width
    )
    hidden_grad = query_grad * query_row + key_grad * key_row + value_grad
    normed_grad = hidden_grad * gain_row
    first_mean = jnp.mean(normed_grad, axis=-1, keepdims=True)
    second_mean = jnp.mean(normed_grad * normed, axis=-1, keepdims=True)
    input_grad = (
        cotangent.astype(jnp.float32) + inverse * (normed_grad - first_mean - normed * second_mean)
    ).astype(jnp.bfloat16)
    sums = jnp.stack(
        [
            jnp.sum(hidden_grad * normed, axis=0),
            jnp.sum(query_grad * hidden, axis=0),
            jnp.sum(key_grad * hidden, axis=0),
        ]
    )
    return (input_grad, sums)


def shards(
    section_inputs,
    norm_gain,
    query_gain,
    key_gain,
    output_weight,
    full_sequence_gradient,
    patch_order,
):
    inputs = section_inputs[0]
    row_count, feature_width = inputs.shape
    image_count = row_count // KEPT
    section = lax.axis_index("section")
    sections = lax.axis_size("section")
    all_images = image_count * lax.axis_size("dp")
    gain_row = norm_gain[0]
    query_row = query_gain[0]
    key_row = key_gain[0]
    weight = lax.all_gather(output_weight[0], "dp", axis=0, tiled=True)
    normed, inverse = normalize(inputs)
    hidden, queries, key_rows, value_rows, softmaxed, mixed = attend_forward(
        normed, gain_row, query_row, key_row, HEADS
    )
    kept = patch_order[:, :KEPT]
    chosen_patches = (
        kept[:, :, None] == jnp.arange(PATCHES, dtype=jnp.int32)[None, None, :]
    ).astype(jnp.bfloat16)
    upper_bound = (
        jnp.einsum(
            "usn,unj->usj",
            chosen_patches,
            full_sequence_gradient,
            preferred_element_type=jnp.float32,
        )
        .astype(jnp.bfloat16)
        .reshape(row_count, feature_width)
    )
    per_unit = image_count // MICRO
    unit_rows = per_unit * KEPT
    unit_count = image_count // per_unit
    step_count = unit_count + sections - 1

    def take_rows(array, unit):
        return lax.dynamic_slice_in_dim(array, unit * unit_rows, unit_rows, 0)

    def take_images(array, unit):
        return lax.dynamic_slice_in_dim(array, unit * per_unit, per_unit, 0)

    def put_rows(array, piece, unit, valid):
        present_value = take_rows(array, unit)
        return lax.dynamic_update_slice_in_dim(
            array, jnp.where(valid, piece, present_value), unit * unit_rows, 0
        )

    def advance(step_index, carry):
        received, cotangents, input_grads, sums, running_weight = carry
        unit = step_index - (sections - 1 - section)
        valid = jnp.logical_and(unit >= 0, unit < unit_count)
        safe_unit = jnp.clip(unit, 0, unit_count - 1)
        cotangent = jnp.where(section == sections - 1, take_rows(upper_bound, safe_unit), received)
        back = lax.dot_general(
            cotangent, weight, (((1,), (1,)), ((), ())), preferred_element_type=jnp.float32
        )
        input_grad, partial_sums = attend_backward(
            cotangent,
            back,
            take_rows(normed, safe_unit),
            take_rows(inverse, safe_unit),
            take_rows(hidden, safe_unit),
            take_images(queries, safe_unit),
            take_images(key_rows, safe_unit),
            take_images(value_rows, safe_unit),
            take_images(softmaxed, safe_unit),
            gain_row,
            query_row,
            key_row,
        )
        cotangents = put_rows(cotangents, cotangent, safe_unit, valid)
        input_grads = put_rows(input_grads, input_grad, safe_unit, valid)
        sums = sums + jnp.where(valid, partial_sums, 0.0)
        received = from_behind(input_grad, "section", -1)
        return (received, cotangents, input_grads, sums, running_weight)

    weight_offset = jnp.zeros((1,), jnp.float32)
    start_carry = (
        jnp.zeros((unit_rows, feature_width), jnp.bfloat16),
        jnp.zeros_like(inputs),
        jnp.zeros_like(inputs),
        jnp.zeros((3, feature_width), jnp.float32),
        weight_offset,
    )
    final_carry = lax.fori_loop(0, step_count, advance, start_carry)
    cotangents = final_carry[1]
    input_grads = final_carry[2]
    gain_total = lax.psum(final_carry[3], "dp") / all_images
    weight_share = (
        lax.psum_scatter(
            lax.dot_general(
                mixed, cotangents, (((0,), (0,)), ((), ())), preferred_element_type=jnp.float32
            ),
            "dp",
            scatter_dimension=0,
            tiled=True,
        )
        / all_images
    )
    return (input_grads[None], weight_share[None], gain_total[None])


def solution(mesh):
    return jax.shard_map(
        shards,
        mesh=mesh,
        in_specs=(
            P("section", "dp", None),
            P("section", None),
            P("section", None),
            P("section", None),
            P("section", "dp", None),
            P("dp", None, None),
            P("dp", None),
        ),
        out_specs=(P("section", "dp", None), P("section", "dp", None), P("section", None, None)),
        check_vma=False,
    )
```

profile of v0, /device:TPU:96, one launch (start us, length us, event | category | flops | bytes accessed | tf_op | source)
XLA Modules:
  0.0 857.8 jit_solution(7415387619002725321)
XLA Ops:
  12.7 4.7 fusion.17
  26.9 4.0 multiply_reduce_fusion.6
  32.1 3.7 fusion.23
  39.3 82.6 %all-gather.3.cloned.1.call-done = bf16[1,2048,2048]{2,1,0:T(8,128)(2,1)} async-done(((bf16[1,32,2048]{2,1,0:T(8,128)(2,1)}), bf16[1,2048,2048]{2,1,0:T(8,128)(2,1)}) %all-gather.3.cloned.1.call-update) | async-done | bytes 8388624 | tf_op jit(solution)/shard_map/all_gather | solution.py:118
  124.6 193.8 %while.22 = (s32[]{:T(128)}, bf16[98,2048]{1,0:T(8,128)(2,1)}, bf16[196,2048]{1,0:T(8,128)(2,1)}, bf16[196,2048]{1,0:T(8,128)(2,1)}, f32[3,2048]{1,0:T(4,128)S(1...) while((s32[]{:T(128)}, bf16[98,2048]{1,0:T(8,128)(2,1)}, ...), condition=%wide.region_11.12_spmd.clone, body=%wide.region_4.11_spmd.clone.sunk | while | flops 1300798208 | bytes 88767504 | solution.py:191
  126.9 6.1 fusion.47
  133.3 3.1 multiply_reduce_fusion.11
  150.6 5.7 collective-permute-start
  156.2 3.3 dynamic_update_slice.22
  159.5 3.3 dynamic_update_slice.23
  167.5 6.1 fusion.47
  173.8 3.1 multiply_reduce_fusion.11
  191.1 5.3 collective-permute-start
  196.4 3.1 dynamic_update_slice.22
  199.6 3.1 dynamic_update_slice.23
  206.9 6.1 fusion.47
  213.2 3.1 multiply_reduce_fusion.11
  230.5 5.3 collective-permute-start
  235.8 3.1 dynamic_update_slice.22
  238.9 3.1 dynamic_update_slice.23
  245.3 6.1 fusion.47
  251.7 3.1 multiply_reduce_fusion.11
  269.0 5.3 collective-permute-start
  274.2 3.1 dynamic_update_slice.22
  277.4 3.1 dynamic_update_slice.23
  283.0 6.1 fusion.47
  306.6 5.3 collective-permute-start
  311.9 3.1 dynamic_update_slice.22
  315.0 3.1 dynamic_update_slice.23
  318.4 9.5 %fusion.30 = f32[2048,2048]{1,0:T(8,128)} fusion(bf16[196,2048]{1,0:T(8,128)(2,1)} %bitcast.137, bf16[196,2048]{1,0:T(8,128)(2,1)} %get-tuple-element.412), kind=kOutput, calls=%fused_computation.62 | convolution fusion | flops 1644167168 | bytes 18382848 | tf_op jit(solution)/shard_map/dot_general | solution.py:197
  328.0 425.0 %psum.7 = f32[3,2048]{1,0:T(4,128)S(1)} all-reduce(f32[3,2048]{1,0:T(4,128)S(1)} %get-tuple-element.413), channel_id=1, replica_groups=mesh['section'=4,'dp'=64] {'dp'}, use_global_device_ids=true, to_apply=%region_13.14 | all-reduce | flops 6144 | bytes 49152 | tf_op jit(solution)/shard_map/psum | solution.py:194
  753.7 95.6 %reduce-scatter.2.cloned.1.call-done = f32[32,2048]{1,0:T(8,128)} async-done(((f32[2048,2048]{1,0:T(8,128)}), f32[32,2048]{1,0:T(8,128)}) %reduce-scatter.2.cloned.1.call-update) | async-done | bytes 262160 | tf_op jit(solution)/shard_map/reduce_scatter | solution.py:196
  (236 shorter events, 115.9 us)
Async XLA Ops:
  7.2 5.5 copy-start
  7.2 114.7 %all-gather.3.cloned.1.call-start = ((), (), s32[]{:S(2)}) async-start(), calls=%async_computation.2 | async-start | bytes 8519680 | tf_op jit(solution)/shard_map/all_gather | solution.py:118
  7.9 841.4 %reduce-scatter.2.cloned.1.call-start = ((), (), s32[]{:S(2)}) async-start(), calls=%async_computation.1 | async-start | bytes 17039360 | tf_op jit(solution)/shard_map/reduce_scatter | solution.py:196
  8.0 2.8 copy-start.8
  8.0 4.7 slice-start
  17.4 2.5 copy-start.11
  21.4 1.8 copy-start.14
  133.2 3.1 copy-start.6
  136.4 1.7 copy-start.5
  146.1 1.9 copy-start.7
  148.7 7.5 copy-start.4
  150.6 14.7 %collective-permute-start = (bf16[98,2048]{1,0:T(8,128)(2,1)}, bf16[98,2048]{1,0:T(8,128)(2,1)}, u32[]{:S(2)}, u32[]{:S(2)}) collective-permute-start(bf16[98,2048]{1,0:T(8,128)(2,1)} %get-tuple-element.688), channel_id=1, source_target_pairs={{64,0},{128,64},{192,128},{65,1},{129,65},{193,129},{66,2},{130,66... | collective-permute-start | bytes 1204232 | tf_op jit(solution)/shard_map/while/body/eval_jaxpr/ppermute | solution.py:17
  173.8 3.1 copy-start.6
  177.0 1.7 copy-start.5
  186.7 1.9 copy-start.7
  189.3 7.2 copy-start.4
  191.1 13.4 %collective-permute-start = (bf16[98,2048]{1,0:T(8,128)(2,1)}, bf16[98,2048]{1,0:T(8,128)(2,1)}, u32[]{:S(2)}, u32[]{:S(2)}) collective-permute-start(bf16[98,2048]{1,0:T(8,128)(2,1)} %get-tuple-element.688), channel_id=1, source_target_pairs={{64,0},{128,64},{192,128},{65,1},{129,65},{193,129},{66,2},{130,66... | collective-permute-start | bytes 1204232 | tf_op jit(solution)/shard_map/while/body/eval_jaxpr/ppermute | solution.py:17
  213.2 3.1 copy-start.6
  226.1 1.9 copy-start.7
  228.6 7.2 copy-start.4
  230.5 12.6 %collective-permute-start = (bf16[98,2048]{1,0:T(8,128)(2,1)}, bf16[98,2048]{1,0:T(8,128)(2,1)}, u32[]{:S(2)}, u32[]{:S(2)}) collective-permute-start(bf16[98,2048]{1,0:T(8,128)(2,1)} %get-tuple-element.688), channel_id=1, source_target_pairs={{64,0},{128,64},{192,128},{65,1},{129,65},{193,129},{66,2},{130,66... | collective-permute-start | bytes 1204232 | tf_op jit(solution)/shard_map/while/body/eval_jaxpr/ppermute | solution.py:17
  251.7 3.1 copy-start.6
  254.8 1.7 copy-start.5
  264.6 1.9 copy-start.7
  267.1 7.2 copy-start.4
  269.0 11.7 %collective-permute-start = (bf16[98,2048]{1,0:T(8,128)(2,1)}, bf16[98,2048]{1,0:T(8,128)(2,1)}, u32[]{:S(2)}, u32[]{:S(2)}) collective-permute-start(bf16[98,2048]{1,0:T(8,128)(2,1)} %get-tuple-element.688), channel_id=1, source_target_pairs={{64,0},{128,64},{192,128},{65,1},{129,65},{193,129},{66,2},{130,66... | collective-permute-start | bytes 1204232 | tf_op jit(solution)/shard_map/while/body/eval_jaxpr/ppermute | solution.py:17
  289.3 3.1 copy-start.6
  292.5 1.7 copy-start.5
  302.2 1.9 copy-start.7
  304.7 7.2 copy-start.4
  306.6 11.6 %collective-permute-start = (bf16[98,2048]{1,0:T(8,128)(2,1)}, bf16[98,2048]{1,0:T(8,128)(2,1)}, u32[]{:S(2)}, u32[]{:S(2)}) collective-permute-start(bf16[98,2048]{1,0:T(8,128)(2,1)} %get-tuple-element.688), channel_id=1, source_target_pairs={{64,0},{128,64},{192,128},{65,1},{129,65},{193,129},{66,2},{130,66... | collective-permute-start | bytes 1204232 | tf_op jit(solution)/shard_map/while/body/eval_jaxpr/ppermute | solution.py:17
  328.0 523.0 %copy-start.1 = (bf16[4,196,2048]{2,0,1:T(4,128)(2,1)S(1)}, bf16[4,196,2048]{2,0,1:T(4,128)(2,1)}, u32[]{:S(2)}) copy-start(bf16[4,196,2048]{2,0,1:T(4,128)(2,1)} %param.14) | copy-start | bytes 9633796
  (19 other events, 25.2 us)
Sparse Core Ops, SparseCore 0:
  11.5 110.3 all-gather.2
  328.1 521.1 reduce-scatter.1
where the time goes:
time: 860 us; the launch traced here: 858 us
  blocking collectives  425 us (49%)
  waiting for transfers between devices  184 us (21%)
  matrix products  95.3 us (11%)
  local copies, waits for them, and re-layouts  80 us (9%)
  other arithmetic  31.3 us (4%)
  starting transfers between devices  26.8 us (3%)
  between operations  14.2 us (2%)
    psum x1, blocking collectives, shards(): gain_total = lax.psum(final_carry[3], 'dp') / all_images  425 us
    reduce_scatter x1, waiting for transfers between devices, shards(): lax.psum_scatter(lax.dot_general(mixed, cotangents, (((0,), (0,)), ((), (...  95.6 us
    all_gather x1, waiting for transfers between devices, shards(): weight = lax.all_gather(output_weight[0], 'dp', axis=0, tiled=True)  82.6 us
    dynamic_update_slice x10, local copies, waits for them, and re-layouts, put_rows(): lax.dynamic_update_slice_in_dim(array, jnp.where(valid, piece, present_va...  31.8 us
    dot_general x5, matrix products, advance(): lax.dot_general(cotangent, weight, (((1,), (1,)), ((), ())), preferred_el...  30.5 us
    ppermute x5, starting transfers between devices, from_behind(): return lax.ppermute(block, axis, route)  26.7 us
    while x110, local copies, waits for them, and re-layouts  22.4 us
    select_n x10, other arithmetic, put_rows(): jnp.where(valid, piece, present_value)  17.9 us
  transfers between devices with their start and end apart: 7, of which 6 were waited for; matrix products, arithmetic and copies ran while one was open for 7% of the time, Pallas kernels for 0%

commit v1 on v0

--- a/solution.py
+++ b/solution.py
@@ -1,3 +1,4 @@
+import functools
 import math
 import jax
 import jax.numpy as jnp
@@ -9,6 +10,13 @@
 PATCHES = 196
 MICRO = 2
 highest = lax.Precision.HIGHEST
+
+
+def hubs_convert(q_in, across):
+    return lax.all_gather(q_in, across).sum(axis=0)
+
+
+track_pools = functools.partial(hubs_convert, across="dp")
 
 
 def from_behind(block, axis, distance):
@@ -191,7 +199,7 @@
     final_carry = lax.fori_loop(0, step_count, advance, start_carry)
     cotangents = final_carry[1]
     input_grads = final_carry[2]
-    gain_total = lax.psum(final_carry[3], "dp") / all_images
+    gain_total = track_pools(final_carry[3]) / all_images
     weight_share = (
         lax.psum_scatter(
             lax.dot_general(

time: 860 us -> 924 us (1.074)
  waiting for transfers between devices: 184 us -> 669 us
  blocking collectives: 425 us -> 0 us
    psum x1 -> x0, blocking collectives: 425 us -> none  [shards(): gain_total = lax.psum(final_carry[3], 'dp') / all_images]
    reduce_scatter x1, waiting for transfers between devices: 95.6 us -> 514 us  [shards(): lax.psum_scatter(lax.dot_general(mixed, cotangents, (((0,), (0,)), ((), (...]
    all_gather x0 -> x1, waiting for transfers between devices: none -> 62.4 us  [hubs_convert(): return lax.all_gather(q_in, across).sum(axis=0)]
  transfers between devices with their start and end apart: 7 -> 8, of which waited for: 6 -> 7; matrix products, arithmetic and copies ran while one was open for 7% -> 8% of each run, Pallas kernels for 0% -> 0%
where the time goes in v1:
time: 924 us; the launch traced here: 922 us
  waiting for transfers between devices  669 us (72%)
  matrix products  96.5 us (10%)
  local copies, waits for them, and re-layouts  80.6 us (9%)
  other arithmetic  33.1 us (4%)
  starting transfers between devices  27 us (3%)
  between operations  13.9 us (2%)
    reduce_scatter x1, waiting for transfers between devices, shards(): lax.psum_scatter(lax.dot_general(mixed, cotangents, (((0,), (0,)), ((), (...  514 us
    all_gather x1, waiting for transfers between devices, shards(): weight = lax.all_gather(output_weight[0], 'dp', axis=0, tiled=True)  87.1 us
    all_gather x1, waiting for transfers between devices, hubs_convert(): return lax.all_gather(q_in, across).sum(axis=0)  62.4 us
    dynamic_update_slice x10, local copies, waits for them, and re-layouts, put_rows(): lax.dynamic_update_slice_in_dim(array, jnp.where(valid, piece, present_va...  31.8 us
    dot_general x5, matrix products, advance(): lax.dot_general(cotangent, weight, (((1,), (1,)), ((), ())), preferred_el...  30.5 us
    ppermute x5, starting transfers between devices, from_behind(): return lax.ppermute(block, axis, route)  26.9 us
    while x110, local copies, waits for them, and re-layouts  22.4 us
  transfers between devices with their start and end apart: 8, of which 7 were waited for; matrix products, arithmetic and copies ran while one was open for 8% of the time, Pallas kernels for 0%

profile of v1, /device:TPU:96, one launch (start us, length us, event | category | flops | bytes accessed | tf_op | source)
XLA Modules:
  0.0 921.6 jit_solution(7106424424973978805)
XLA Ops:
  12.6 4.7 fusion.17
  26.9 4.0 multiply_reduce_fusion.6
  34.8 87.1 %all-gather.6.cloned.1.call-done = bf16[1,2048,2048]{2,1,0:T(8,128)(2,1)} async-done(((bf16[1,32,2048]{2,1,0:T(8,128)(2,1)}), bf16[1,2048,2048]{2,1,0:T(8,128)(2,1)}) %all-gather.6.cloned.1.call-update) | async-done | bytes 8388624 | tf_op jit(solution)/shard_map/all_gather | solution.py:126
  124.6 194.2 %while.22 = (s32[]{:T(128)}, bf16[98,2048]{1,0:T(8,128)(2,1)}, bf16[196,2048]{1,0:T(8,128)(2,1)}, bf16[196,2048]{1,0:T(8,128)(2,1)}, f32[3,2048]{1,0:T(4,128)S(1...) while((s32[]{:T(128)}, bf16[98,2048]{1,0:T(8,128)(2,1)}, ...), condition=%wide.region_11.12_spmd.clone, body=%wide.region_4.11_spmd.clone.sunk | while | flops 1300798208 | bytes 88767504 | solution.py:199
  126.9 6.1 fusion.47
  133.2 3.1 multiply_reduce_fusion.11
  150.6 5.7 collective-permute-start
  156.3 3.3 dynamic_update_slice.22
  159.6 3.3 dynamic_update_slice.23
  167.6 6.1 fusion.47
  173.9 3.1 multiply_reduce_fusion.11
  191.2 5.3 collective-permute-start
  196.6 3.1 dynamic_update_slice.22
  199.7 3.1 dynamic_update_slice.23
  207.0 6.1 fusion.47
  230.7 5.3 collective-permute-start
  236.0 3.1 dynamic_update_slice.22
  239.1 3.1 dynamic_update_slice.23
  245.6 6.1 fusion.47
  251.9 3.2 multiply_reduce_fusion.11
  269.3 5.3 collective-permute-start
  274.6 3.1 dynamic_update_slice.22
  277.7 3.1 dynamic_update_slice.23
  283.3 6.1 fusion.47
  289.6 3.2 multiply_reduce_fusion.11
  307.0 5.3 collective-permute-start
  312.3 3.1 dynamic_update_slice.22
  315.4 3.1 dynamic_update_slice.23
  319.5 5.1 fusion.23
  325.1 9.3 %fusion.30 = f32[2048,2048]{1,0:T(8,128)} fusion(bf16[196,2048]{1,0:T(8,128)(2,1)S(1)} %bitcast.138, bf16[196,2048]{1,0:T(8,128)(2,1)} %get-tuple-element.412), kind=kOutput, calls=%fused_computation.62 | convolution fusion | flops 1644167168 | bytes 18382848 | tf_op jit(solution)/shard_map/dot_general | solution.py:205
  334.4 62.4 %all-gather.8.cloned.1.call-done = f32[64,3,2048]{2,1,0:T(4,128)} async-done(((f32[1,3,2048]{2,1,0:T(4,128)}), f32[64,3,2048]{2,1,0:T(4,128)}) %all-gather.8.cloned.1.call-update) | async-done | bytes 1572880 | tf_op jit(solution)/shard_map/all_gather | solution.py:16
  399.4 514.0 %reduce-scatter.2.cloned.1.call-done = f32[32,2048]{1,0:T(8,128)} async-done(((f32[2048,2048]{1,0:T(8,128)}), f32[32,2048]{1,0:T(8,128)}) %reduce-scatter.2.cloned.1.call-update) | async-done | bytes 262160 | tf_op jit(solution)/shard_map/reduce_scatter | solution.py:204
  (243 shorter events, 118.2 us)
Async XLA Ops:
  7.2 5.5 copy-start
  7.2 114.6 %all-gather.6.cloned.1.call-start = ((), (), s32[]{:S(2)}) async-start(), calls=%async_computation.2 | async-start | bytes 8519680 | tf_op jit(solution)/shard_map/all_gather | solution.py:126
  7.9 388.9 %all-gather.8.cloned.1.call-start = ((), (), s32[]{:S(2)}) async-start(), calls=%async_computation.3 | async-start | bytes 2129920 | tf_op jit(solution)/shard_map/all_gather | solution.py:16
  8.0 2.8 copy-start.9
  8.0 4.6 slice-start
  17.4 2.4 copy-start.12
  21.3 1.9 copy-start.5
  21.3 1.8 copy-start.16
  133.2 3.1 copy-start.7
  136.4 1.7 copy-start.6
  146.1 1.9 copy-start.8
  148.7 7.6 copy-start.4
  150.6 14.7 %collective-permute-start = (bf16[98,2048]{1,0:T(8,128)(2,1)}, bf16[98,2048]{1,0:T(8,128)(2,1)}, u32[]{:S(2)}, u32[]{:S(2)}) collective-permute-start(bf16[98,2048]{1,0:T(8,128)(2,1)} %get-tuple-element.707), channel_id=1, source_target_pairs={{64,0},{128,64},{192,128},{65,1},{129,65},{193,129},{66,2},{130,66... | collective-permute-start | bytes 1204232 | tf_op jit(solution)/shard_map/while/body/eval_jaxpr/ppermute | solution.py:25
  173.9 3.1 copy-start.7
  177.0 1.7 copy-start.6
  186.8 1.9 copy-start.8
  189.4 7.2 copy-start.4
  191.2 13.5 %collective-permute-start = (bf16[98,2048]{1,0:T(8,128)(2,1)}, bf16[98,2048]{1,0:T(8,128)(2,1)}, u32[]{:S(2)}, u32[]{:S(2)}) collective-permute-start(bf16[98,2048]{1,0:T(8,128)(2,1)} %get-tuple-element.707), channel_id=1, source_target_pairs={{64,0},{128,64},{192,128},{65,1},{129,65},{193,129},{66,2},{130,66... | collective-permute-start | bytes 1204232 | tf_op jit(solution)/shard_map/while/body/eval_jaxpr/ppermute | solution.py:25
  213.3 3.1 copy-start.7
  226.3 1.9 copy-start.8
  228.8 7.2 copy-start.4
  230.7 12.6 %collective-permute-start = (bf16[98,2048]{1,0:T(8,128)(2,1)}, bf16[98,2048]{1,0:T(8,128)(2,1)}, u32[]{:S(2)}, u32[]{:S(2)}) collective-permute-start(bf16[98,2048]{1,0:T(8,128)(2,1)} %get-tuple-element.707), channel_id=1, source_target_pairs={{64,0},{128,64},{192,128},{65,1},{129,65},{193,129},{66,2},{130,66... | collective-permute-start | bytes 1204232 | tf_op jit(solution)/shard_map/while/body/eval_jaxpr/ppermute | solution.py:25
  251.9 3.2 copy-start.7
  264.9 1.9 copy-start.8
  267.4 7.2 copy-start.4
  269.3 11.7 %collective-permute-start = (bf16[98,2048]{1,0:T(8,128)(2,1)}, bf16[98,2048]{1,0:T(8,128)(2,1)}, u32[]{:S(2)}, u32[]{:S(2)}) collective-permute-start(bf16[98,2048]{1,0:T(8,128)(2,1)} %get-tuple-element.707), channel_id=1, source_target_pairs={{64,0},{128,64},{192,128},{65,1},{129,65},{193,129},{66,2},{130,66... | collective-permute-start | bytes 1204232 | tf_op jit(solution)/shard_map/while/body/eval_jaxpr/ppermute | solution.py:25
  289.6 3.2 copy-start.7
  302.6 1.9 copy-start.8
  305.1 7.2 copy-start.4
  307.0 11.6 %collective-permute-start = (bf16[98,2048]{1,0:T(8,128)(2,1)}, bf16[98,2048]{1,0:T(8,128)(2,1)}, u32[]{:S(2)}, u32[]{:S(2)}) collective-permute-start(bf16[98,2048]{1,0:T(8,128)(2,1)} %get-tuple-element.707), channel_id=1, source_target_pairs={{64,0},{128,64},{192,128},{65,1},{129,65},{193,129},{66,2},{130,66... | collective-permute-start | bytes 1204232 | tf_op jit(solution)/shard_map/while/body/eval_jaxpr/ppermute | solution.py:25
  319.5 593.9 %reduce-scatter.2.cloned.1.call-start = ((), (), s32[]{:S(2)}) async-start(), calls=%async_computation.1 | async-start | bytes 17039360 | tf_op jit(solution)/shard_map/reduce_scatter | solution.py:204
  334.4 580.6 %copy-start.1 = (bf16[4,196,2048]{2,0,1:T(4,128)(2,1)S(1)}, bf16[4,196,2048]{2,0,1:T(4,128)(2,1)}, u32[]{:S(2)}) copy-start(bf16[4,196,2048]{2,0,1:T(4,128)(2,1)} %param.14) | copy-start | bytes 9633796
  (22 other events, 29.1 us)
Sparse Core Ops, SparseCore 0:
  11.5 110.3 all-gather.5
  319.6 77.1 all-gather.7
  399.4 513.9 reduce-scatter.1
